TPU v7x, 256 devices: a whole 4x4x8 slice. The times are simulated.
256 devices in a mesh: lat: 16 (over y_lo, x, core), lon: 16 (over y_hi, z).
Axes of the slice: x: 4, y: 4 (y_hi: 2, y_lo: 2; y = y_hi * 2 + y_lo), z: 8, core: 2. Of those that a mesh axis runs over, the one named last changes fastest.
Arguments:
- fields: bfloat16 [32, 128, 4096], P(None, 'lat', 'lon'), may hold values from -6 to 6
- cotangent: bfloat16 [32, 128, 4096], P(None, 'lat', 'lon'), may hold values from -0.008239746 to 0.008239746
- kernel_in: bfloat16 [9, 128, 32], replicated, may hold values from -0.375 to 0.375
- kernel_mid: bfloat16 [9, 128, 128], replicated, may hold values from -0.1875 to 0.1875
- kernel_out: bfloat16 [9, 32, 128], replicated, may hold values from -0.1875 to 0.1875
- patch_anchors: int32 [16, 16, 4, 2], P('lat', 'lon'), may hold values from 0 to 8
- blend_weights: int32 [4, 128, 4096], P(None, 'lat', 'lon'), may hold values from 1 to 8
- tile_counts: int32 [16, 16], P('lat', 'lon'), may hold values from 0 to 4, as said below
Outputs:
- blended: float32 [32, 128, 4096], P(None, 'lat', 'lon')
- grad_in: float32 [9, 128, 32], replicated
- grad_mid: float32 [9, 128, 128], replicated
- grad_out: float32 [9, 32, 128], replicated
Inputs may be any that keep to these rules, and one draw needn't show every extreme that they name: `tile_counts`: the counts of the tiles in lat rows i and i + 8 at the same lon sum to exactly 4; tile (1, 0) holds 4 patches and tile (9, 0) none.
All inputs are finite; a program needn't handle non-finite values.
Results may differ from a plain program's by a relative error of at most 0.005.
Values may be sent and summed in bfloat16 or wider, within the bound.
A program may use at most 64 MiB of HBM per device.

v0:
```python
import jax
import jax.numpy as jnp
from jax import lax
from jax.sharding import PartitionSpec as P

MARGIN = 4
SLOTS = 4
KERNEL_TAPS = ((0, 0), (0, 1), (0, 2), (1, 0), (1, 1), (1, 2), (2, 0), (2, 1), (2, 2))


def extended_2(block, sides, width):
    for axis, dim in sides:
        count = lax.axis_size(axis)
        forward = [(i, i + 1) for i in range(count - 1)]
        forward.append((count - 1, 0))
        backward = [(target, source) for source, target in forward]
        low = lax.ppermute(
            lax.slice_in_dim(block, block.shape[dim] - width, None, axis=dim), axis, forward
        )
        high = lax.ppermute(lax.slice_in_dim(block, 0, width, axis=dim), axis, backward)
        block = jnp.concatenate([low, block, high], axis=dim)
    return block


def shifted(value, axis, steps):
    count = lax.axis_size(axis)
    pairs = [(source, (source + steps) % count) for source in range(count)]
    return lax.ppermute(value, axis, pairs)


def forward_conv(values, kernel):
    height, breadth = (values.shape[1], values.shape[2])
    padded = jnp.pad(values, ((0, 0), (1, 1), (1, 1)))
    summed = jnp.zeros((kernel.shape[1], height, breadth), jnp.float32)
    for tap_index, (tap_row, tap_col) in enumerate(KERNEL_TAPS):
        summed = summed + jnp.einsum(
            "ok,khw->ohw",
            kernel[tap_index],
            padded[:, tap_row : tap_row + height, tap_col : tap_col + breadth],
            preferred_element_type=jnp.float32,
        )
    return summed


def backward_conv(cotangent, kernel):
    height, breadth = (cotangent.shape[1], cotangent.shape[2])
    padded = jnp.pad(cotangent, ((0, 0), (1, 1), (1, 1)))
    summed = jnp.zeros((kernel.shape[2], height, breadth), jnp.float32)
    for tap_index, (tap_row, tap_col) in enumerate(KERNEL_TAPS):
        summed = summed + jnp.einsum(
            "ok,ohw->khw",
            kernel[tap_index],
            padded[:, 2 - tap_row : 2 - tap_row + height, 2 - tap_col : 2 - tap_col + breadth],
            preferred_element_type=jnp.float32,
        )
    return summed


def kernel_grad(cotangent, values):
    height, breadth = (values.shape[1], values.shape[2])
    padded = jnp.pad(values, ((0, 0), (1, 1), (1, 1)))
    pieces = [
        jnp.einsum(
            "ohw,khw->ok",
            cotangent,
            padded[:, tap_row : tap_row + height, tap_col : tap_col + breadth],
            preferred_element_type=jnp.float32,
        )
        for tap_row, tap_col in KERNEL_TAPS
    ]
    return jnp.stack(pieces)


def silu_slope(pre_act):
    sigmoid = jax.nn.sigmoid(pre_act)
    return sigmoid * (1.0 + pre_act * (1.0 - sigmoid))


def patch_pass(inputs, out_grad, kernel_in, kernel_mid, kernel_out):
    pre_one = forward_conv(inputs, kernel_in)
    hidden_one = jax.nn.silu(pre_one).astype(jnp.bfloat16)
    pre_two = forward_conv(hidden_one, kernel_mid)
    hidden_two = (hidden_one.astype(jnp.float32) + jax.nn.silu(pre_two)).astype(jnp.bfloat16)
    result = forward_conv(hidden_two, kernel_out)
    grad_two = backward_conv(out_grad, kernel_out)
    delta_two = (grad_two * silu_slope(pre_two)).astype(jnp.bfloat16)
    grad_one = grad_two + backward_conv(delta_two, kernel_mid)
    delta_one = (grad_one * silu_slope(pre_one)).astype(jnp.bfloat16)
    return (
        result,
        kernel_grad(delta_one, inputs),
        kernel_grad(delta_two, hidden_one),
        kernel_grad(out_grad, hidden_two),
    )


def run_patches(inputs, out_grads, kernel_in, kernel_mid, kernel_out):
    initial = (
        jnp.zeros(kernel_in.shape, jnp.float32),
        jnp.zeros(kernel_mid.shape, jnp.float32),
        jnp.zeros(kernel_out.shape, jnp.float32),
    )

    def step_patch(running, slot_pair):
        result, part_in, part_mid, part_out = patch_pass(
            slot_pair[0], slot_pair[1], kernel_in, kernel_mid, kernel_out
        )
        return ((running[0] + part_in, running[1] + part_mid, running[2] + part_out), result)

    return lax.scan(step_patch, initial, (inputs, out_grads))


def fold_canvas(canvas, keep_top, keep_bottom):
    extended = extended_2(canvas, (("lat", 1), ("lon", 2)), MARGIN)
    height = canvas.shape[1] - 2 * MARGIN
    breadth = canvas.shape[2] - 2 * MARGIN
    inner_rows = slice(2 * MARGIN, 2 * MARGIN + height)
    inner_cols = slice(2 * MARGIN, 2 * MARGIN + breadth)
    center_part = extended[:, inner_rows, inner_cols]
    col_left = ((0, 0), (0, 0), (0, breadth - MARGIN))
    col_right = ((0, 0), (0, 0), (breadth - MARGIN, 0))
    upper_part = (
        extended[:, :MARGIN, inner_cols]
        + jnp.pad(extended[:, :MARGIN, :MARGIN], col_left)
        + jnp.pad(extended[:, :MARGIN, -MARGIN:], col_right)
    )
    lower_part = (
        extended[:, -MARGIN:, inner_cols]
        + jnp.pad(extended[:, -MARGIN:, :MARGIN], col_left)
        + jnp.pad(extended[:, -MARGIN:, -MARGIN:], col_right)
    )
    summed = (
        center_part
        + jnp.pad(extended[:, inner_rows, :MARGIN], col_left)
        + jnp.pad(extended[:, inner_rows, -MARGIN:], col_right)
    )
    summed = summed + jnp.pad(upper_part * keep_top, ((0, 0), (0, height - MARGIN), (0, 0)))
    summed = summed + jnp.pad(lower_part * keep_bottom, ((0, 0), (height - MARGIN, 0), (0, 0)))
    return summed


def shards(
    fields, cotangent, kernel_in, kernel_mid, kernel_out, patch_anchors, blend_weights, tile_counts
):
    channels, height, breadth = (fields.shape[0], fields.shape[1], fields.shape[2])
    canvas_rows = height + 2 * MARGIN
    canvas_cols = breadth + 2 * MARGIN
    lat_size = lax.axis_size("lat")
    lat_index = lax.axis_index("lat")
    keep_top = (lat_index > 0).astype(jnp.float32)
    keep_bottom = (lat_index < lat_size - 1).astype(jnp.float32)
    slot_count = tile_counts[0, 0]
    slot_live = (jnp.arange(SLOTS) < slot_count).astype(jnp.int32)
    weights = (blend_weights * slot_live[:, None, None]).astype(jnp.float32)
    starts = patch_anchors[0, 0]

    def place_slots(per_slot):
        canvas = jnp.zeros((per_slot.shape[1], canvas_rows, canvas_cols), jnp.float32)
        for slot_index in range(SLOTS):
            corner = (jnp.int32(0), starts[slot_index, 0], starts[slot_index, 1])
            current = lax.dynamic_slice(canvas, corner, per_slot.shape[1:])
            canvas = lax.dynamic_update_slice(canvas, current + per_slot[slot_index], corner)
        return canvas

    total_weight = jnp.maximum(
        fold_canvas(place_slots(weights[:, None]), keep_top, keep_bottom), 1.0
    )
    scaled = (cotangent.astype(jnp.float32) / total_weight).astype(jnp.bfloat16)
    wide_fields, wide_scaled = (
        extended_2(fields, (("lat", 1), ("lon", 2)), MARGIN),
        extended_2(scaled, (("lat", 1), ("lon", 2)), MARGIN),
    )
    row_ids = jnp.arange(canvas_rows)[None, :, None]
    keep_rows = ((row_ids >= MARGIN) | (keep_top > 0.0)) & (
        (row_ids < height + MARGIN) | (keep_bottom > 0.0)
    )
    wide_fields = jnp.where(keep_rows, wide_fields, jnp.zeros_like(wide_fields))
    wide_scaled = jnp.where(keep_rows, wide_scaled, jnp.zeros_like(wide_scaled))
    window_list = []
    grad_list = []
    for slot_index in range(SLOTS):
        corner = (jnp.int32(0), starts[slot_index, 0], starts[slot_index, 1])
        window_list.append(lax.dynamic_slice(wide_fields, corner, (channels, height, breadth)))
        scaled_window = lax.dynamic_slice(wide_scaled, corner, (channels, height, breadth)).astype(
            jnp.float32
        )
        grad_list.append((weights[slot_index] * scaled_window).astype(jnp.bfloat16))
    inputs = jnp.stack(window_list)
    out_grads = jnp.stack(grad_list)
    half_slots = SLOTS // 2
    upper_half = (lat_index >= lat_size // 2).astype(jnp.int32)
    first_count = jnp.where(upper_half == 0, slot_count, SLOTS - slot_count)
    outgoing_inputs = jnp.where(upper_half == 0, inputs[half_slots:], inputs[:half_slots])
    outgoing_grads = jnp.where(upper_half == 0, out_grads[half_slots:], out_grads[:half_slots])
    incoming_inputs, incoming_grads = shifted(
        (outgoing_inputs, outgoing_grads), "lat", lat_size // 2
    )
    table_inputs = jnp.concatenate([inputs, incoming_inputs], axis=0)
    table_grads = jnp.concatenate([out_grads, incoming_grads], axis=0)
    position = upper_half * half_slots + jnp.arange(half_slots, dtype=jnp.int32)
    picked = jnp.where(
        position < first_count,
        jnp.where(upper_half == 0, position, position + SLOTS - half_slots),
        jnp.where(upper_half == 0, SLOTS + position - first_count, position - first_count),
    )
    picked = jnp.clip(picked, 0, SLOTS + half_slots - 1)
    totals, computed = run_patches(
        jnp.take(table_inputs, picked, axis=0),
        jnp.take(table_grads, picked, axis=0),
        kernel_in,
        kernel_mid,
        kernel_out,
    )
    returned = shifted(computed, "lat", lat_size // 2)
    ordered = jnp.where(
        upper_half == 0,
        jnp.concatenate([computed, returned], axis=0),
        jnp.concatenate([returned, computed], axis=0),
    )
    where_slot = jnp.clip(
        jnp.arange(SLOTS, dtype=jnp.int32) + upper_half * first_count, 0, SLOTS - 1
    )
    outputs = jnp.take(ordered, where_slot, axis=0)
    weighted = weights[:, None] * outputs
    numerator = fold_canvas(place_slots(weighted), keep_top, keep_bottom)
    blended = numerator / total_weight
    summed_grads = lax.psum((totals[0], totals[1], totals[2]), ("lat", "lon"))
    return (blended, summed_grads[0], summed_grads[1], summed_grads[2])


def solution(mesh):
    return jax.shard_map(
        shards,
        mesh=mesh,
        in_specs=(
            P(None, "lat", "lon"),
            P(None, "lat", "lon"),
            P(),
            P(),
            P(),
            P("lat", "lon", None, None),
            P(None, "lat", "lon"),
            P("lat", "lon"),
        ),
        out_specs=(P(None, "lat", "lon"), P(), P(), P()),
        check_vma=False,
    )
```

profile of v0, /device:TPU:1, one launch (start us, length us, event | category | flops | bytes accessed | tf_op | source)
XLA Modules:
  0.0 498.2 jit_solution(12220531734381858021)
XLA Ops:
  22.0 0.8 dynamic_update_slice.31
  22.9 0.8 dynamic_update_slice.32
  27.7 2.6 collective-permute-start
  30.3 0.8 collective-permute-start.1
  31.2 3.8 collective-permute-start.10
  35.4 7.0 %collective-permute-start.3 = (f32[1,24,4]{2,1,0:T(8,128)S(1)}, f32[1,24,4]{2,1,0:T(8,128)S(1)}, u32[]{:S(2)}, u32[]{:S(2)}) collective-permute-start(f32[1,24,4]{2,1,0:T(8,128)S(1)} %get-tuple-element.254), channel_id=1, source_target_pairs={{1,0},{2,1},{3,2},{4,3},{5,4},{6,5},{7,6},{8,7},{9,8},{10,9},{11,1... | collective-permute-start | bytes 1160 | tf_op jit(solution)/shard_map/ppermute | solution.py:20
  42.4 1.0 collective-permute-done.2
  46.1 5.5 %collective-permute-start.12 = (bf16[32,16,4]{2,1,0:T(8,128)(2,1)S(1)}, bf16[32,16,4]{2,1,0:T(8,128)(2,1)S(1)}, u32[]{:S(2)}, u32[]{:S(2)}) collective-permute-start(bf16[32,16,4]{2,1,0:T(8,128)(2,1)S(1)} %get-tuple-element.246), channel_id=1, source_target_pairs={{1,0},{2,1},{3,2},{4,3},{5,4},{6,5},{7,6},{8,7},{9,8},{10,9},{11,1... | collective-permute-start | bytes 12296 | tf_op jit(solution)/shard_map/ppermute | solution.py:20
  52.0 18.8 %collective-permute-start.7 = (bf16[32,16,4]{2,1,0:T(8,128)(2,1)S(1)}, bf16[32,16,4]{2,1,0:T(8,128)(2,1)S(1)}, u32[]{:S(2)}, u32[]{:S(2)}) collective-permute-start(bf16[32,16,4]{2,1,0:T(8,128)(2,1)S(1)} %get-tuple-element.248), channel_id=1, source_target_pairs={{1,0},{2,1},{3,2},{4,3},{5,4},{6,5},{7,6},{8,7},{9,8},{10,9},{11,1... | collective-permute-start | bytes 12296 | tf_op jit(solution)/shard_map/ppermute | solution.py:20
  70.8 1.9 collective-permute-done.7
  72.7 1.0 maximum_select_fusion.2
  74.5 0.8 collective-permute-start.8
  75.8 0.8 collective-permute-start.13
  76.7 3.1 collective-permute-done.8
  80.4 2.2 collective-permute-done.13
  83.2 0.8 broadcast_select_fusion
  84.2 72.5 %while.19 = (s32[]{:T(128)}, f32[9,128,32]{1,2,0:T(8,128)S(1)}, f32[9,128,128]{2,1,0:T(8,128)S(1)}, f32[9,32,128]{2,1,0:T(8,128)}, f32[2,32,8,256]{3,2,1,0:T(8,1...) while((s32[]{:T(128)}, f32[9,128,32]{1,2,0:T(8,128)S(1)}, ...), condition=%wide.region_1.3_spmd.clone, body=%wide.region_0.2_spmd.clone.sunk | while | flops 2583609344 | bytes 133587216 | solution.py:110
  84.2 1.0 constant_dynamic-slice_fusion.3
  88.7 1.6 multiply_convert_fusion.8
  96.6 0.8 add_convert_fusion.2
  99.9 0.8 copy-done.8
  100.9 0.8 fusion.448
  101.8 0.8 fusion.449
  102.6 0.8 fusion.450
  103.4 0.9 fusion.451
  104.3 0.8 fusion.452
  105.1 0.9 fusion.453
  105.9 0.8 fusion.454
  106.8 0.8 fusion.455
  107.6 0.8 fusion.456
  108.5 1.6 select_add_fusion.8
  115.7 0.9 copy-done.20
  119.5 0.9 copy-done.5
  120.4 1.0 constant_dynamic-slice_fusion.3
  124.9 1.6 multiply_convert_fusion.8
  132.9 0.8 add_convert_fusion.2
  136.2 0.8 copy-done.8
  137.1 0.8 fusion.448
  138.0 0.8 fusion.449
  138.8 0.8 fusion.450
  139.6 0.9 fusion.451
  140.5 0.8 fusion.452
  141.3 0.9 fusion.453
  142.2 0.8 fusion.454
  143.0 0.8 fusion.455
  143.8 0.8 fusion.456
  144.7 1.7 select_add_fusion.8
  152.0 0.9 copy-done.20
  155.8 0.9 copy-done.5
  157.5 7.5 %collective-permute-done.14 = f32[2,32,8,256]{3,2,1,0:T(8,128)S(1)} collective-permute-done((f32[2,32,8,256]{3,2,1,0:T(8,128)}, f32[2,32,8,256]{3,2,1,0:T(8,128)S(1)}, u32[]{:S(2)}, u32[]{:S(2)}) %collective-permute-start.14) | collective-permute-done | bytes 524320 | tf_op jit(solution)/shard_map/ppermute | solution.py:28
  165.0 1.3 maximum_select_fusion
  167.3 10.2 %dynamic_update_slice.35 = f32[32,16,264]{2,1,0:T(8,128)S(1)} dynamic-update-slice(f32[32,16,264]{2,1,0:T(8,128)S(1)} %broadcast_in_dim.59, f32[32,8,256]{2,1,0:T(8,128)S(1)} %slice_bitcast_fusion.3, s32[]{:T(128)} %constant.84.clone.1, s32[]{:T(128)S(6)} %select_n.136, s32[]{:T(128)S(6)} %select_n.137) | dynamic-update-slice | bytes 524292 | tf_op jit(solution)/shard_map/dynamic_update_slice | solution.py:162
  177.6 10.2 %dynamic_update_slice.36 = f32[32,16,264]{2,1,0:T(8,128)S(1)} dynamic-update-slice(f32[32,16,264]{2,1,0:T(8,128)S(1)} %dynamic_update_slice.35, f32[32,8,256]{2,1,0:T(8,128)S(1)} %fusion.200, s32[]{:T(128)} %constant.84.clone.1, s32[]{:T(128)S(6)} %select_n.138, s32[]{:T(128)S(6)} %select_n.139) | dynamic-update-slice | bytes 524292 | tf_op jit(solution)/shard_map/dynamic_update_slice | solution.py:162
  188.0 1.3 dynamic_update_slice.37
  189.4 10.2 %dynamic_update_slice.38 = f32[32,16,264]{2,1,0:T(8,128)S(1)} dynamic-update-slice(f32[32,16,264]{2,1,0:T(8,128)S(1)} %dynamic_update_slice.37, f32[32,8,256]{2,1,0:T(8,128)S(1)} %fusion.198, s32[]{:T(128)} %constant.84.clone.1, s32[]{:T(128)S(6)} %select_n.142, s32[]{:T(128)S(6)} %select_n.143) | dynamic-update-slice | bytes 524292 | tf_op jit(solution)/shard_map/dynamic_update_slice | solution.py:162
  199.6 9.2 %collective-permute-start.15 = (f32[32,4,264]{2,1,0:T(4,128)S(1)}, f32[32,4,264]{2,1,0:T(4,128)S(1)}, u32[]{:S(2)}, u32[]{:S(2)}) collective-permute-start(f32[32,4,264]{2,1,0:T(4,128)S(1)} %get-tuple-element.239), channel_id=1, source_target_pairs={{0,16},{16,32},{32,48},{48,64},{64,80},{80,96},{96,112},{112,128},... | collective-permute-start | bytes 405512 | tf_op jit(solution)/shard_map/ppermute | solution.py:17
  208.8 2.6 collective-permute-done.15
  211.4 6.6 %collective-permute-done.16 = f32[32,4,264]{2,1,0:T(4,128)S(1)} collective-permute-done((f32[32,4,264]{2,1,0:T(4,128)S(1)}, f32[32,4,264]{2,1,0:T(4,128)S(1)}, u32[]{:S(2)}, u32[]{:S(2)}) %collective-permute-start.16) | collective-permute-done | bytes 135200 | tf_op jit(solution)/shard_map/ppermute | solution.py:20
  218.4 11.1 %collective-permute-start.18 = (f32[32,24,4]{2,1,0:T(8,128)S(1)}, f32[32,24,4]{2,1,0:T(8,128)S(1)}, u32[]{:S(2)}, u32[]{:S(2)}) collective-permute-start(f32[32,24,4]{2,1,0:T(8,128)S(1)} %get-tuple-element.238), channel_id=1, source_target_pairs={{1,0},{2,1},{3,2},{4,3},{5,4},{6,5},{7,6},{8,7},{9,8},{10,9},{11,1... | collective-permute-start | bytes 36872 | tf_op jit(solution)/shard_map/ppermute | solution.py:20
  229.4 5.5 %collective-permute-done.17 = f32[32,24,4]{2,1,0:T(8,128)S(1)} collective-permute-done((f32[32,24,4]{2,1,0:T(8,128)S(1)}, f32[32,24,4]{2,1,0:T(8,128)S(1)}, u32[]{:S(2)}, u32[]{:S(2)}) %collective-permute-start.17) | collective-permute-done | bytes 12320 | tf_op jit(solution)/shard_map/ppermute | solution.py:17
  237.6 0.9 fusion.197
  238.5 248.2 %all-reduce.24.cloned.1.call-done = (f32[9,128,32]{1,2,0:T(8,128)}, f32[9,128,128]{2,1,0:T(8,128)}, f32[9,32,128]{2,1,0:T(8,128)}) async-done(((f32[9,128,32]{1,2,0:T(8,128)}, f32[9,128,128]{2,1,0:T(8,128)}, f32[9,32,128]{2,1,0:T(8,128)}), (f32[9,128,32]{1,2,0:T(8,128)}, f32[9,128,128]{2,1,0:T(8,128)}, f32[9,32,128]{2,1,0:T(8,128)})) %all-reduce.24.cloned.1.call-update) | async-done | bytes 884752 | tf_op jit(solution)/shard_map/psum | solution.py:227
  486.7 1.6 copy.283
  488.3 2.0 copy.284
  (267 shorter events, 56.3 us)
Async XLA Ops:
  7.2 0.7 copy-start.19
  7.2 479.6 %all-reduce.24.cloned.1.call-start = ((), (), s32[]{:S(2)}) async-start(), calls=%async_computation | async-start | bytes 1769472 | tf_op jit(solution)/shard_map/psum | solution.py:227
  8.5 10.9 %copy-start.18 = (s32[4,8,256]{2,1,0:T(8,128)S(1)}, s32[4,8,256]{2,1,0:T(8,128)}, u32[]{:S(2)}) copy-start(s32[4,8,256]{2,1,0:T(8,128)} %param.18) | copy-start | bytes 98308
  19.4 7.4 %copy-start.12 = (f32[4,8,256]{2,1,0:T(8,128)}, f32[4,8,256]{2,1,0:T(8,128)S(1)}, u32[]{:S(2)}) copy-start(f32[4,8,256]{2,1,0:T(8,128)S(1)} %multiply_convert_fusion.6) | copy-start | bytes 98308
  22.0 9.1 %copy-start.7 = (bf16[32,8,256]{2,1,0:T(8,128)(2,1)S(1)}, bf16[32,8,256]{2,1,0:T(8,128)(2,1)}, u32[]{:S(2)}) copy-start(bf16[32,8,256]{2,1,0:T(8,128)(2,1)} %param.12) | copy-start | bytes 393220
  27.7 7.3 %collective-permute-start = (f32[1,4,264]{2,1,0:T(4,128)S(1)}, f32[1,4,264]{2,1,0:T(4,128)S(1)}, u32[]{:S(2)}, u32[]{:S(2)}) collective-permute-start(f32[1,4,264]{2,1,0:T(4,128)S(1)} %get-tuple-element.260), channel_id=1, source_target_pairs={{0,16},{16,32},{32,48},{48,64},{64,80},{80,96},{96,112},{112,128},... | collective-permute-start | bytes 12680 | tf_op jit(solution)/shard_map/ppermute | solution.py:17
  30.3 4.7 collective-permute-start.1
  31.2 12.5 %copy-start.15 = (bf16[32,8,256]{2,1,0:T(8,128)(2,1)S(1)}, bf16[32,8,256]{2,1,0:T(8,128)(2,1)}, u32[]{:S(2)}) copy-start(bf16[32,8,256]{2,1,0:T(8,128)(2,1)} %param.13) | copy-start | bytes 393220
  31.2 14.6 %collective-permute-start.10 = (bf16[32,4,256]{2,1,0:T(4,128)(2,1)S(1)}, bf16[32,4,256]{2,1,0:T(4,128)(2,1)S(1)}, u32[]{:S(2)}, u32[]{:S(2)}) collective-permute-start(bf16[32,4,256]{2,1,0:T(4,128)(2,1)S(1)} %get-tuple-element.250), channel_id=1, source_target_pairs={{16,0},{32,16},{48,32},{64,48},{80,64},{96,80},{112,96},{128,112},... | collective-permute-start | bytes 196616 | tf_op jit(solution)/shard_map/ppermute | solution.py:20
  35.0 10.7 %collective-permute-start.9 = (bf16[32,4,256]{2,1,0:T(4,128)(2,1)S(1)}, bf16[32,4,256]{2,1,0:T(4,128)(2,1)S(1)}, u32[]{:S(2)}, u32[]{:S(2)}) collective-permute-start(bf16[32,4,256]{2,1,0:T(4,128)(2,1)S(1)} %get-tuple-element.249), channel_id=1, source_target_pairs={{0,16},{16,32},{32,48},{48,64},{64,80},{80,96},{96,112},{112,128},... | collective-permute-start | bytes 196616 | tf_op jit(solution)/shard_map/ppermute | solution.py:17
  35.1 8.3 %collective-permute-start.2 = (f32[1,24,4]{2,1,0:T(8,128)S(1)}, f32[1,24,4]{2,1,0:T(8,128)S(1)}, u32[]{:S(2)}, u32[]{:S(2)}) collective-permute-start(f32[1,24,4]{2,1,0:T(8,128)S(1)} %get-tuple-element.253), channel_id=1, source_target_pairs={{0,1},{1,2},{2,3},{3,4},{4,5},{5,6},{6,7},{7,8},{8,9},{9,10},{10,1... | collective-permute-start | bytes 1160 | tf_op jit(solution)/shard_map/ppermute | solution.py:17
  35.4 8.0 %collective-permute-start.3 = (f32[1,24,4]{2,1,0:T(8,128)S(1)}, f32[1,24,4]{2,1,0:T(8,128)S(1)}, u32[]{:S(2)}, u32[]{:S(2)}) collective-permute-start(f32[1,24,4]{2,1,0:T(8,128)S(1)} %get-tuple-element.254), channel_id=1, source_target_pairs={{1,0},{2,1},{3,2},{4,3},{5,4},{6,5},{7,6},{8,7},{9,8},{10,9},{11,1... | collective-permute-start | bytes 1160 | tf_op jit(solution)/shard_map/ppermute | solution.py:20
  43.6 0.6 copy-start.16
  44.3 7.3 %collective-permute-start.4 = (bf16[32,4,256]{2,1,0:T(4,128)(2,1)S(1)}, bf16[32,4,256]{2,1,0:T(4,128)(2,1)S(1)}, u32[]{:S(2)}, u32[]{:S(2)}) collective-permute-start(bf16[32,4,256]{2,1,0:T(4,128)(2,1)S(1)} %get-tuple-element.251), channel_id=1, source_target_pairs={{0,16},{16,32},{32,48},{48,64},{64,80},{80,96},{96,112},{112,128},... | collective-permute-start | bytes 196616 | tf_op jit(solution)/shard_map/ppermute | solution.py:17
  45.0 6.6 %collective-permute-start.5 = (bf16[32,4,256]{2,1,0:T(4,128)(2,1)S(1)}, bf16[32,4,256]{2,1,0:T(4,128)(2,1)S(1)}, u32[]{:S(2)}, u32[]{:S(2)}) collective-permute-start(bf16[32,4,256]{2,1,0:T(4,128)(2,1)S(1)} %get-tuple-element.252), channel_id=1, source_target_pairs={{16,0},{32,16},{48,32},{64,48},{80,64},{96,80},{112,96},{128,112},... | collective-permute-start | bytes 196616 | tf_op jit(solution)/shard_map/ppermute | solution.py:20
  46.0 24.8 %collective-permute-start.11 = (bf16[32,16,4]{2,1,0:T(8,128)(2,1)S(1)}, bf16[32,16,4]{2,1,0:T(8,128)(2,1)S(1)}, u32[]{:S(2)}, u32[]{:S(2)}) collective-permute-start(bf16[32,16,4]{2,1,0:T(8,128)(2,1)S(1)} %get-tuple-element.245), channel_id=1, source_target_pairs={{0,1},{1,2},{2,3},{3,4},{4,5},{5,6},{6,7},{7,8},{8,9},{9,10},{10,1... | collective-permute-start | bytes 12296 | tf_op jit(solution)/shard_map/ppermute | solution.py:17
  46.1 24.7 %collective-permute-start.12 = (bf16[32,16,4]{2,1,0:T(8,128)(2,1)S(1)}, bf16[32,16,4]{2,1,0:T(8,128)(2,1)S(1)}, u32[]{:S(2)}, u32[]{:S(2)}) collective-permute-start(bf16[32,16,4]{2,1,0:T(8,128)(2,1)S(1)} %get-tuple-element.246), channel_id=1, source_target_pairs={{1,0},{2,1},{3,2},{4,3},{5,4},{6,5},{7,6},{8,7},{9,8},{10,9},{11,1... | collective-permute-start | bytes 12296 | tf_op jit(solution)/shard_map/ppermute | solution.py:20
  51.9 18.9 %collective-permute-start.6 = (bf16[32,16,4]{2,1,0:T(8,128)(2,1)S(1)}, bf16[32,16,4]{2,1,0:T(8,128)(2,1)S(1)}, u32[]{:S(2)}, u32[]{:S(2)}) collective-permute-start(bf16[32,16,4]{2,1,0:T(8,128)(2,1)S(1)} %get-tuple-element.247), channel_id=1, source_target_pairs={{0,1},{1,2},{2,3},{3,4},{4,5},{5,6},{6,7},{7,8},{8,9},{9,10},{10,1... | collective-permute-start | bytes 12296 | tf_op jit(solution)/shard_map/ppermute | solution.py:17
  52.0 20.8 %collective-permute-start.7 = (bf16[32,16,4]{2,1,0:T(8,128)(2,1)S(1)}, bf16[32,16,4]{2,1,0:T(8,128)(2,1)S(1)}, u32[]{:S(2)}, u32[]{:S(2)}) collective-permute-start(bf16[32,16,4]{2,1,0:T(8,128)(2,1)S(1)} %get-tuple-element.248), channel_id=1, source_target_pairs={{1,0},{2,1},{3,2},{4,3},{5,4},{6,5},{7,6},{8,7},{9,8},{10,9},{11,1... | collective-permute-start | bytes 12296 | tf_op jit(solution)/shard_map/ppermute | solution.py:20
  74.5 5.3 %collective-permute-start.8 = (bf16[2,32,8,256]{3,2,1,0:T(8,128)(2,1)S(1)}, bf16[2,32,8,256]{3,2,1,0:T(8,128)(2,1)S(1)}, u32[]{:S(2)}, u32[]{:S(2)}) collective-permute-start(bf16[2,32,8,256]{3,2,1,0:T(8,128)(2,1)S(1)} %maximum_select_fusion.3), channel_id=1, source_target_pairs={{0,128},{16,144},{32,160},{48,176},{64,192},{80,208},{96,224},{112... | collective-permute-start | bytes 786440 | tf_op jit(solution)/shard_map/ppermute | solution.py:28
  75.8 6.8 %collective-permute-start.13 = (bf16[2,32,8,256]{3,2,1,0:T(8,128)(2,1)S(1)}, bf16[2,32,8,256]{3,2,1,0:T(8,128)(2,1)S(1)}, u32[]{:S(2)}, u32[]{:S(2)}) collective-permute-start(bf16[2,32,8,256]{3,2,1,0:T(8,128)(2,1)S(1)} %maximum_select_fusion.4), channel_id=1, source_target_pairs={{0,128},{16,144},{32,160},{48,176},{64,192},{80,208},{96,224},{112... | collective-permute-start | bytes 786440 | tf_op jit(solution)/shard_map/ppermute | solution.py:28
  83.2 1.0 copy-start
  83.2 1.0 copy-start.2
  83.2 1.0 copy-start.6
  84.2 1.0 copy-start.4
  99.7 1.0 copy-start.8
  100.9 4.2 copy-start.9
  115.4 1.2 copy-start.20
  119.5 1.0 copy-start.5
  120.4 1.0 copy-start.4
  135.9 1.0 copy-start.8
  137.1 4.2 copy-start.9
  151.7 1.2 copy-start.20
  155.8 1.0 copy-start.5
  156.7 9.6 %copy-start.1 = (f32[9,128,128]{2,1,0:T(8,128)}, f32[9,128,128]{2,1,0:T(8,128)S(1)}, u32[]{:S(2)}) copy-start(f32[9,128,128]{2,1,0:T(8,128)S(1)} %get-tuple-element.135) | copy-start | bytes 1769476
  156.7 9.6 %copy-start.3 = (f32[9,128,32]{1,2,0:T(8,128)}, f32[9,128,32]{1,2,0:T(8,128)S(1)}, u32[]{:S(2)}) copy-start(f32[9,128,32]{1,2,0:T(8,128)S(1)} %get-tuple-element.134) | copy-start | bytes 442372
  156.7 8.2 %collective-permute-start.14 = (f32[2,32,8,256]{3,2,1,0:T(8,128)}, f32[2,32,8,256]{3,2,1,0:T(8,128)S(1)}, u32[]{:S(2)}, u32[]{:S(2)}) collective-permute-start(f32[2,32,8,256]{3,2,1,0:T(8,128)} %get-tuple-element.133), channel_id=1, source_target_pairs={{0,128},{16,144},{32,160},{48,176},{64,192},{80,208},{96,224},{112... | collective-permute-start | bytes 1572872 | tf_op jit(solution)/shard_map/ppermute | solution.py:28
  166.3 0.8 copy-start.13
  199.6 11.8 %collective-permute-start.15 = (f32[32,4,264]{2,1,0:T(4,128)S(1)}, f32[32,4,264]{2,1,0:T(4,128)S(1)}, u32[]{:S(2)}, u32[]{:S(2)}) collective-permute-start(f32[32,4,264]{2,1,0:T(4,128)S(1)} %get-tuple-element.239), channel_id=1, source_target_pairs={{0,16},{16,32},{32,48},{48,64},{64,80},{80,96},{96,112},{112,128},... | collective-permute-start | bytes 405512 | tf_op jit(solution)/shard_map/ppermute | solution.py:17
  208.8 9.2 %collective-permute-start.16 = (f32[32,4,264]{2,1,0:T(4,128)S(1)}, f32[32,4,264]{2,1,0:T(4,128)S(1)}, u32[]{:S(2)}, u32[]{:S(2)}) collective-permute-start(f32[32,4,264]{2,1,0:T(4,128)S(1)} %get-tuple-element.240), channel_id=1, source_target_pairs={{16,0},{32,16},{48,32},{64,48},{80,64},{96,80},{112,96},{128,112},... | collective-permute-start | bytes 405512 | tf_op jit(solution)/shard_map/ppermute | solution.py:20
  218.3 16.7 %collective-permute-start.17 = (f32[32,24,4]{2,1,0:T(8,128)S(1)}, f32[32,24,4]{2,1,0:T(8,128)S(1)}, u32[]{:S(2)}, u32[]{:S(2)}) collective-permute-start(f32[32,24,4]{2,1,0:T(8,128)S(1)} %get-tuple-element.237), channel_id=1, source_target_pairs={{0,1},{1,2},{2,3},{3,4},{4,5},{5,6},{6,7},{7,8},{8,9},{9,10},{10,1... | collective-permute-start | bytes 36872 | tf_op jit(solution)/shard_map/ppermute | solution.py:17
  218.4 17.4 %collective-permute-start.18 = (f32[32,24,4]{2,1,0:T(8,128)S(1)}, f32[32,24,4]{2,1,0:T(8,128)S(1)}, u32[]{:S(2)}, u32[]{:S(2)}) collective-permute-start(f32[32,24,4]{2,1,0:T(8,128)S(1)} %get-tuple-element.238), channel_id=1, source_target_pairs={{1,0},{2,1},{3,2},{4,3},{5,4},{6,5},{7,6},{8,7},{9,8},{10,9},{11,1... | collective-permute-start | bytes 36872 | tf_op jit(solution)/shard_map/ppermute | solution.py:20
  235.0 0.8 copy-start.10
  235.7 0.7 copy-start.11
  236.7 0.9 slice-start
  236.7 1.0 slice-start.1
  236.7 1.0 copy-start.17
  488.3 2.0 copy-start.14
Sparse Core Ops, SparseCore 0:
  218.5 268.2 all-reduce.23
where the time goes:
time: 507 us; the launch traced here: 498 us
  waiting for transfers between devices  279 us (55%)
  starting transfers between devices  63.2 us (12%)
  matrix products  60.3 us (12%)
  local copies, waits for them, and re-layouts  53.6 us (11%)
  between operations  30.9 us (6%)
  other arithmetic  10.7 us (2%)
    psum x1, waiting for transfers between devices, shards(): summed_grads = lax.psum((totals[0], totals[1], totals[2]), ('lat', 'lon'))  248 us
    ppermute x8, starting transfers between devices, extended_2(): lax.ppermute(lax.slice_in_dim(block, 0, width, axis=dim), axis, backward)  47.8 us
    dynamic_update_slice x8, local copies, waits for them, and re-layouts, place_slots(): lax.dynamic_update_slice(canvas, current + per_slot[slot_index], corner)  34.6 us
    dot_general x54, matrix products, kernel_grad(): jnp.einsum('ohw,khw->ok', cotangent, padded[:, tap_row:tap_row + height,...  25.4 us
    dot_general x54, matrix products, forward_conv(): jnp.einsum('ok,khw->ohw', kernel[tap_index], padded[:, tap_row:tap_row +...  21.3 us
    dot_general x36, matrix products, backward_conv(): jnp.einsum('ok,ohw->khw', kernel[tap_index], padded[:, 2 - tap_row:2 - ta...  13.6 us
    ppermute x8, starting transfers between devices, extended_2(): lax.ppermute(lax.slice_in_dim(block, block.shape[dim] - width, None, axis...  13 us
    ppermute x3, waiting for transfers between devices, shifted(): return lax.ppermute(value, axis, pairs)  12.8 us
  transfers between devices with their start and end apart: 20, of which 9 were waited for; matrix products, arithmetic and copies ran while one was open for 1% of the time, Pallas kernels for 0%

commit v1 on v0

--- a/solution.py
+++ b/solution.py
@@ -224,7 +224,7 @@
     weighted = weights[:, None] * outputs
     numerator = fold_canvas(place_slots(weighted), keep_top, keep_bottom)
     blended = numerator / total_weight
-    summed_grads = lax.psum((totals[0], totals[1], totals[2]), ("lat", "lon"))
+    summed_grads = lax.psum(lax.psum((totals[0], totals[1], totals[2]), "lon"), "lat")
     return (blended, summed_grads[0], summed_grads[1], summed_grads[2])
 
 

time: 507 us -> 470 us (0.927)
  waiting for transfers between devices: 279 us -> 244 us
    psum x1 -> x2, waiting for transfers between devices: 248 us -> 212 us  [the longest x1 135 us: shards(): lax.psum(lax.psum((totals[0], totals[1], totals[2]), 'lon'), 'lat')]
  transfers between devices with their start and end apart: 20 -> 21, of which waited for: 9 -> 10; matrix products, arithmetic and copies ran while one was open for 1% -> 8% of each run, Pallas kernels for 0% -> 0%
where the time goes in v1:
time: 470 us; the launch traced here: 462 us
  waiting for transfers between devices  244 us (52%)
  starting transfers between devices  63.4 us (13%)
  matrix products  60.3 us (13%)
  local copies, waits for them, and re-layouts  52.9 us (11%)
  between operations  31 us (7%)
  other arithmetic  9.5 us (2%)
    psum x1, waiting for transfers between devices, shards(): lax.psum(lax.psum((totals[0], totals[1], totals[2]), 'lon'), 'lat')  135 us
    psum x1, waiting for transfers between devices, shards(): lax.psum((totals[0], totals[1], totals[2]), 'lon')  77.1 us
    ppermute x8, starting transfers between devices, extended_2(): lax.ppermute(lax.slice_in_dim(block, 0, width, axis=dim), axis, backward)  47.8 us
    dynamic_update_slice x8, local copies, waits for them, and re-layouts, place_slots(): lax.dynamic_update_slice(canvas, current + per_slot[slot_index], corner)  34.6 us
    dot_general x54, matrix products, kernel_grad(): jnp.einsum('ohw,khw->ok', cotangent, padded[:, tap_row:tap_row + height,...  25.4 us
    dot_general x54, matrix products, forward_conv(): jnp.einsum('ok,khw->ohw', kernel[tap_index], padded[:, tap_row:tap_row +...  21.3 us
    dot_general x36, matrix products, backward_conv(): jnp.einsum('ok,ohw->khw', kernel[tap_index], padded[:, 2 - tap_row:2 - ta...  13.6 us
    ppermute x8, starting transfers between devices, extended_2(): lax.ppermute(lax.slice_in_dim(block, block.shape[dim] - width, None, axis...  13 us
  transfers between devices with their start and end apart: 21, of which 10 were waited for; matrix products, arithmetic and copies ran while one was open for 8% of the time, Pallas kernels for 0%

profile of v1, /device:TPU:1, one launch (start us, length us, event | category | flops | bytes accessed | tf_op | source)
XLA Modules:
  0.0 461.6 jit_solution(6065262429663827356)
XLA Ops:
  22.2 0.8 dynamic_update_slice.31
  27.9 2.6 collective-permute-start
  30.5 0.8 collective-permute-start.1
  31.3 3.8 collective-permute-start.10
  35.5 7.0 %collective-permute-start.3 = (f32[1,24,4]{2,1,0:T(8,128)S(1)}, f32[1,24,4]{2,1,0:T(8,128)S(1)}, u32[]{:S(2)}, u32[]{:S(2)}) collective-permute-start(f32[1,24,4]{2,1,0:T(8,128)S(1)} %get-tuple-element.257), channel_id=1, source_target_pairs={{1,0},{2,1},{3,2},{4,3},{5,4},{6,5},{7,6},{8,7},{9,8},{10,9},{11,1... | collective-permute-start | bytes 1160 | tf_op jit(solution)/shard_map/ppermute | solution.py:20
  42.5 1.0 collective-permute-done.2
  46.3 5.5 %collective-permute-start.12 = (bf16[32,16,4]{2,1,0:T(8,128)(2,1)S(1)}, bf16[32,16,4]{2,1,0:T(8,128)(2,1)S(1)}, u32[]{:S(2)}, u32[]{:S(2)}) collective-permute-start(bf16[32,16,4]{2,1,0:T(8,128)(2,1)S(1)} %get-tuple-element.249), channel_id=1, source_target_pairs={{1,0},{2,1},{3,2},{4,3},{5,4},{6,5},{7,6},{8,7},{9,8},{10,9},{11,1... | collective-permute-start | bytes 12296 | tf_op jit(solution)/shard_map/ppermute | solution.py:20
  52.1 18.8 %collective-permute-start.7 = (bf16[32,16,4]{2,1,0:T(8,128)(2,1)S(1)}, bf16[32,16,4]{2,1,0:T(8,128)(2,1)S(1)}, u32[]{:S(2)}, u32[]{:S(2)}) collective-permute-start(bf16[32,16,4]{2,1,0:T(8,128)(2,1)S(1)} %get-tuple-element.251), channel_id=1, source_target_pairs={{1,0},{2,1},{3,2},{4,3},{5,4},{6,5},{7,6},{8,7},{9,8},{10,9},{11,1... | collective-permute-start | bytes 12296 | tf_op jit(solution)/shard_map/ppermute | solution.py:20
  71.0 1.9 collective-permute-done.7
  72.9 1.0 maximum_select_fusion.2
  74.6 0.8 collective-permute-start.8
  76.0 0.8 collective-permute-start.13
  76.9 3.1 collective-permute-done.8
  80.5 2.2 collective-permute-done.13
  83.4 0.8 broadcast_select_fusion
  84.4 72.5 %while.19 = (s32[]{:T(128)}, f32[9,128,32]{1,2,0:T(8,128)S(1)}, f32[9,128,128]{2,1,0:T(8,128)S(1)}, f32[9,32,128]{2,1,0:T(8,128)}, f32[2,32,8,256]{3,2,1,0:T(8,1...) while((s32[]{:T(128)}, f32[9,128,32]{1,2,0:T(8,128)S(1)}, ...), condition=%wide.region_1.3_spmd.clone, body=%wide.region_0.2_spmd.clone.sunk | while | flops 2583609344 | bytes 133587216 | solution.py:110
  84.4 1.0 constant_dynamic-slice_fusion.3
  88.8 1.5 multiply_convert_fusion.8
  96.8 0.8 add_convert_fusion.2
  100.1 0.8 copy-done.8
  101.1 0.8 fusion.448
  101.9 0.8 fusion.449
  102.7 0.8 fusion.450
  103.6 0.9 fusion.451
  104.4 0.8 fusion.452
  105.2 0.9 fusion.453
  106.1 0.8 fusion.454
  107.0 0.8 fusion.455
  107.8 0.8 fusion.456
  108.6 1.6 select_add_fusion.8
  115.9 0.9 copy-done.21
  119.7 0.9 copy-done.5
  120.6 1.0 constant_dynamic-slice_fusion.3
  125.0 1.5 multiply_convert_fusion.8
  133.0 0.8 add_convert_fusion.2
  136.3 0.8 copy-done.8
  137.3 0.8 fusion.448
  138.1 0.8 fusion.449
  138.9 0.8 fusion.450
  139.8 0.9 fusion.451
  140.7 0.8 fusion.452
  141.5 0.9 fusion.453
  142.3 0.8 fusion.454
  143.2 0.8 fusion.455
  144.0 0.8 fusion.456
  144.8 1.7 select_add_fusion.8
  152.2 0.9 copy-done.21
  156.0 0.9 copy-done.5
  156.9 0.8 collective-permute-start.14
  157.9 7.4 %collective-permute-done.14 = f32[2,32,8,256]{3,2,1,0:T(8,128)S(1)} collective-permute-done((f32[2,32,8,256]{3,2,1,0:T(8,128)}, f32[2,32,8,256]{3,2,1,0:T(8,128)S(1)}, u32[]{:S(2)}, u32[]{:S(2)}) %collective-permute-start.14) | collective-permute-done | bytes 524320 | tf_op jit(solution)/shard_map/ppermute | solution.py:28
  166.3 10.2 %dynamic_update_slice.35 = f32[32,16,264]{2,1,0:T(8,128)S(1)} dynamic-update-slice(f32[32,16,264]{2,1,0:T(8,128)S(1)} %broadcast_in_dim.59, f32[32,8,256]{2,1,0:T(8,128)S(1)} %slice_bitcast_fusion.3, s32[]{:T(128)} %constant.84.clone.1, s32[]{:T(128)S(6)} %select_n.136, s32[]{:T(128)S(6)} %select_n.137) | dynamic-update-slice | bytes 524292 | tf_op jit(solution)/shard_map/dynamic_update_slice | solution.py:162
  176.6 10.2 %dynamic_update_slice.36 = f32[32,16,264]{2,1,0:T(8,128)S(1)} dynamic-update-slice(f32[32,16,264]{2,1,0:T(8,128)S(1)} %dynamic_update_slice.35, f32[32,8,256]{2,1,0:T(8,128)S(1)} %fusion.200, s32[]{:T(128)} %constant.84.clone.1, s32[]{:T(128)S(6)} %select_n.138, s32[]{:T(128)S(6)} %select_n.139) | dynamic-update-slice | bytes 524292 | tf_op jit(solution)/shard_map/dynamic_update_slice | solution.py:162
  187.0 1.3 dynamic_update_slice.37
  188.4 10.2 %dynamic_update_slice.38 = f32[32,16,264]{2,1,0:T(8,128)S(1)} dynamic-update-slice(f32[32,16,264]{2,1,0:T(8,128)S(1)} %dynamic_update_slice.37, f32[32,8,256]{2,1,0:T(8,128)S(1)} %fusion.198, s32[]{:T(128)} %constant.84.clone.1, s32[]{:T(128)S(6)} %select_n.142, s32[]{:T(128)S(6)} %select_n.143) | dynamic-update-slice | bytes 524292 | tf_op jit(solution)/shard_map/dynamic_update_slice | solution.py:162
  198.6 9.2 %collective-permute-start.15 = (f32[32,4,264]{2,1,0:T(4,128)S(1)}, f32[32,4,264]{2,1,0:T(4,128)S(1)}, u32[]{:S(2)}, u32[]{:S(2)}) collective-permute-start(f32[32,4,264]{2,1,0:T(4,128)S(1)} %get-tuple-element.242), channel_id=1, source_target_pairs={{0,16},{16,32},{32,48},{48,64},{64,80},{80,96},{96,112},{112,128},... | collective-permute-start | bytes 405512 | tf_op jit(solution)/shard_map/ppermute | solution.py:17
  207.8 2.6 collective-permute-done.15
  210.4 6.6 %collective-permute-done.16 = f32[32,4,264]{2,1,0:T(4,128)S(1)} collective-permute-done((f32[32,4,264]{2,1,0:T(4,128)S(1)}, f32[32,4,264]{2,1,0:T(4,128)S(1)}, u32[]{:S(2)}, u32[]{:S(2)}) %collective-permute-start.16) | collective-permute-done | bytes 135200 | tf_op jit(solution)/shard_map/ppermute | solution.py:20
  217.4 11.1 %collective-permute-start.18 = (f32[32,24,4]{2,1,0:T(8,128)S(1)}, f32[32,24,4]{2,1,0:T(8,128)S(1)}, u32[]{:S(2)}, u32[]{:S(2)}) collective-permute-start(f32[32,24,4]{2,1,0:T(8,128)S(1)} %get-tuple-element.241), channel_id=1, source_target_pairs={{1,0},{2,1},{3,2},{4,3},{5,4},{6,5},{7,6},{8,7},{9,8},{10,9},{11,1... | collective-permute-start | bytes 36872 | tf_op jit(solution)/shard_map/ppermute | solution.py:20
  228.5 7.0 %collective-permute-done.17 = f32[32,24,4]{2,1,0:T(8,128)S(1)} collective-permute-done((f32[32,24,4]{2,1,0:T(8,128)S(1)}, f32[32,24,4]{2,1,0:T(8,128)S(1)}, u32[]{:S(2)}, u32[]{:S(2)}) %collective-permute-start.17) | collective-permute-done | bytes 12320 | tf_op jit(solution)/shard_map/ppermute | solution.py:17
  236.4 77.1 %all-reduce.26.cloned.1.call-done = (f32[9,128,32]{1,2,0:T(8,128)}, f32[9,128,128]{2,1,0:T(8,128)}, f32[9,32,128]{2,1,0:T(8,128)}) async-done(((f32[9,128,32]{1,2,0:T(8,128)}, f32[9,128,128]{2,1,0:T(8,128)}, f32[9,32,128]{2,1,0:T(8,128)}), (f32[9,128,32]{1,2,0:T(8,128)}, f32[9,128,128]{2,1,0:T(8,128)}, f32[9,32,128]{2,1,0:T(8,128)})) %all-reduce.26.cloned.1.call-update) | async-done | bytes 884752 | tf_op jit(solution)/shard_map/psum | solution.py:227
  314.6 0.9 fusion.197
  315.5 134.6 %all-reduce.28.cloned.1.call-done = (f32[9,128,32]{1,2,0:T(8,128)}, f32[9,128,128]{2,1,0:T(8,128)}, f32[9,32,128]{2,1,0:T(8,128)}) async-done(((f32[9,128,32]{1,2,0:T(8,128)}, f32[9,128,128]{2,1,0:T(8,128)}, f32[9,32,128]{2,1,0:T(8,128)}), (f32[9,128,32]{1,2,0:T(8,128)}, f32[9,128,128]{2,1,0:T(8,128)}, f32[9,32,128]{2,1,0:T(8,128)})) %all-reduce.28.cloned.1.call-update) | async-done | bytes 884752 | tf_op jit(solution)/shard_map/psum | solution.py:227
  450.1 1.6 copy.286
  451.7 2.0 copy.287
  (272 shorter events, 55.9 us)
Async XLA Ops:
  7.2 0.7 copy-start.20
  7.2 306.2 %all-reduce.26.cloned.1.call-start = ((), (), s32[]{:S(2)}) async-start(), calls=%async_computation | async-start | bytes 1769472 | tf_op jit(solution)/shard_map/psum | solution.py:227
  8.5 10.9 %copy-start.19 = (s32[4,8,256]{2,1,0:T(8,128)S(1)}, s32[4,8,256]{2,1,0:T(8,128)}, u32[]{:S(2)}) copy-start(s32[4,8,256]{2,1,0:T(8,128)} %param.18) | copy-start | bytes 98308
  19.6 7.5 %copy-start.13 = (f32[4,8,256]{2,1,0:T(8,128)}, f32[4,8,256]{2,1,0:T(8,128)S(1)}, u32[]{:S(2)}) copy-start(f32[4,8,256]{2,1,0:T(8,128)S(1)} %multiply_convert_fusion.6) | copy-start | bytes 98308
  22.2 9.1 %copy-start.7 = (bf16[32,8,256]{2,1,0:T(8,128)(2,1)S(1)}, bf16[32,8,256]{2,1,0:T(8,128)(2,1)}, u32[]{:S(2)}) copy-start(bf16[32,8,256]{2,1,0:T(8,128)(2,1)} %param.12) | copy-start | bytes 393220
  27.9 7.3 %collective-permute-start = (f32[1,4,264]{2,1,0:T(4,128)S(1)}, f32[1,4,264]{2,1,0:T(4,128)S(1)}, u32[]{:S(2)}, u32[]{:S(2)}) collective-permute-start(f32[1,4,264]{2,1,0:T(4,128)S(1)} %get-tuple-element.263), channel_id=1, source_target_pairs={{0,16},{16,32},{32,48},{48,64},{64,80},{80,96},{96,112},{112,128},... | collective-permute-start | bytes 12680 | tf_op jit(solution)/shard_map/ppermute | solution.py:17
  30.5 4.7 %collective-permute-start.1 = (f32[1,4,264]{2,1,0:T(4,128)S(1)}, f32[1,4,264]{2,1,0:T(4,128)S(1)}, u32[]{:S(2)}, u32[]{:S(2)}) collective-permute-start(f32[1,4,264]{2,1,0:T(4,128)S(1)} %get-tuple-element.264), channel_id=1, source_target_pairs={{16,0},{32,16},{48,32},{64,48},{80,64},{96,80},{112,96},{128,112},... | collective-permute-start | bytes 12680 | tf_op jit(solution)/shard_map/ppermute | solution.py:20
  31.3 12.5 %copy-start.16 = (bf16[32,8,256]{2,1,0:T(8,128)(2,1)S(1)}, bf16[32,8,256]{2,1,0:T(8,128)(2,1)}, u32[]{:S(2)}) copy-start(bf16[32,8,256]{2,1,0:T(8,128)(2,1)} %param.13) | copy-start | bytes 393220
  31.3 14.6 %collective-permute-start.10 = (bf16[32,4,256]{2,1,0:T(4,128)(2,1)S(1)}, bf16[32,4,256]{2,1,0:T(4,128)(2,1)S(1)}, u32[]{:S(2)}, u32[]{:S(2)}) collective-permute-start(bf16[32,4,256]{2,1,0:T(4,128)(2,1)S(1)} %get-tuple-element.253), channel_id=1, source_target_pairs={{16,0},{32,16},{48,32},{64,48},{80,64},{96,80},{112,96},{128,112},... | collective-permute-start | bytes 196616 | tf_op jit(solution)/shard_map/ppermute | solution.py:20
  35.2 10.8 %collective-permute-start.9 = (bf16[32,4,256]{2,1,0:T(4,128)(2,1)S(1)}, bf16[32,4,256]{2,1,0:T(4,128)(2,1)S(1)}, u32[]{:S(2)}, u32[]{:S(2)}) collective-permute-start(bf16[32,4,256]{2,1,0:T(4,128)(2,1)S(1)} %get-tuple-element.252), channel_id=1, source_target_pairs={{0,16},{16,32},{32,48},{48,64},{64,80},{80,96},{96,112},{112,128},... | collective-permute-start | bytes 196616 | tf_op jit(solution)/shard_map/ppermute | solution.py:17
  35.2 8.3 %collective-permute-start.2 = (f32[1,24,4]{2,1,0:T(8,128)S(1)}, f32[1,24,4]{2,1,0:T(8,128)S(1)}, u32[]{:S(2)}, u32[]{:S(2)}) collective-permute-start(f32[1,24,4]{2,1,0:T(8,128)S(1)} %get-tuple-element.256), channel_id=1, source_target_pairs={{0,1},{1,2},{2,3},{3,4},{4,5},{5,6},{6,7},{7,8},{8,9},{9,10},{10,1... | collective-permute-start | bytes 1160 | tf_op jit(solution)/shard_map/ppermute | solution.py:17
  35.5 8.0 %collective-permute-start.3 = (f32[1,24,4]{2,1,0:T(8,128)S(1)}, f32[1,24,4]{2,1,0:T(8,128)S(1)}, u32[]{:S(2)}, u32[]{:S(2)}) collective-permute-start(f32[1,24,4]{2,1,0:T(8,128)S(1)} %get-tuple-element.257), channel_id=1, source_target_pairs={{1,0},{2,1},{3,2},{4,3},{5,4},{6,5},{7,6},{8,7},{9,8},{10,9},{11,1... | collective-permute-start | bytes 1160 | tf_op jit(solution)/shard_map/ppermute | solution.py:20
  43.8 0.6 copy-start.17
  44.4 7.3 %collective-permute-start.4 = (bf16[32,4,256]{2,1,0:T(4,128)(2,1)S(1)}, bf16[32,4,256]{2,1,0:T(4,128)(2,1)S(1)}, u32[]{:S(2)}, u32[]{:S(2)}) collective-permute-start(bf16[32,4,256]{2,1,0:T(4,128)(2,1)S(1)} %get-tuple-element.254), channel_id=1, source_target_pairs={{0,16},{16,32},{32,48},{48,64},{64,80},{80,96},{96,112},{112,128},... | collective-permute-start | bytes 196616 | tf_op jit(solution)/shard_map/ppermute | solution.py:17
  45.2 6.6 %collective-permute-start.5 = (bf16[32,4,256]{2,1,0:T(4,128)(2,1)S(1)}, bf16[32,4,256]{2,1,0:T(4,128)(2,1)S(1)}, u32[]{:S(2)}, u32[]{:S(2)}) collective-permute-start(bf16[32,4,256]{2,1,0:T(4,128)(2,1)S(1)} %get-tuple-element.255), channel_id=1, source_target_pairs={{16,0},{32,16},{48,32},{64,48},{80,64},{96,80},{112,96},{128,112},... | collective-permute-start | bytes 196616 | tf_op jit(solution)/shard_map/ppermute | solution.py:20
  46.2 24.8 %collective-permute-start.11 = (bf16[32,16,4]{2,1,0:T(8,128)(2,1)S(1)}, bf16[32,16,4]{2,1,0:T(8,128)(2,1)S(1)}, u32[]{:S(2)}, u32[]{:S(2)}) collective-permute-start(bf16[32,16,4]{2,1,0:T(8,128)(2,1)S(1)} %get-tuple-element.248), channel_id=1, source_target_pairs={{0,1},{1,2},{2,3},{3,4},{4,5},{5,6},{6,7},{7,8},{8,9},{9,10},{10,1... | collective-permute-start | bytes 12296 | tf_op jit(solution)/shard_map/ppermute | solution.py:17
  46.3 24.7 %collective-permute-start.12 = (bf16[32,16,4]{2,1,0:T(8,128)(2,1)S(1)}, bf16[32,16,4]{2,1,0:T(8,128)(2,1)S(1)}, u32[]{:S(2)}, u32[]{:S(2)}) collective-permute-start(bf16[32,16,4]{2,1,0:T(8,128)(2,1)S(1)} %get-tuple-element.249), channel_id=1, source_target_pairs={{1,0},{2,1},{3,2},{4,3},{5,4},{6,5},{7,6},{8,7},{9,8},{10,9},{11,1... | collective-permute-start | bytes 12296 | tf_op jit(solution)/shard_map/ppermute | solution.py:20
  52.0 18.9 %collective-permute-start.6 = (bf16[32,16,4]{2,1,0:T(8,128)(2,1)S(1)}, bf16[32,16,4]{2,1,0:T(8,128)(2,1)S(1)}, u32[]{:S(2)}, u32[]{:S(2)}) collective-permute-start(bf16[32,16,4]{2,1,0:T(8,128)(2,1)S(1)} %get-tuple-element.250), channel_id=1, source_target_pairs={{0,1},{1,2},{2,3},{3,4},{4,5},{5,6},{6,7},{7,8},{8,9},{9,10},{10,1... | collective-permute-start | bytes 12296 | tf_op jit(solution)/shard_map/ppermute | solution.py:17
  52.1 20.8 %collective-permute-start.7 = (bf16[32,16,4]{2,1,0:T(8,128)(2,1)S(1)}, bf16[32,16,4]{2,1,0:T(8,128)(2,1)S(1)}, u32[]{:S(2)}, u32[]{:S(2)}) collective-permute-start(bf16[32,16,4]{2,1,0:T(8,128)(2,1)S(1)} %get-tuple-element.251), channel_id=1, source_target_pairs={{1,0},{2,1},{3,2},{4,3},{5,4},{6,5},{7,6},{8,7},{9,8},{10,9},{11,1... | collective-permute-start | bytes 12296 | tf_op jit(solution)/shard_map/ppermute | solution.py:20
  74.6 5.3 %collective-permute-start.8 = (bf16[2,32,8,256]{3,2,1,0:T(8,128)(2,1)S(1)}, bf16[2,32,8,256]{3,2,1,0:T(8,128)(2,1)S(1)}, u32[]{:S(2)}, u32[]{:S(2)}) collective-permute-start(bf16[2,32,8,256]{3,2,1,0:T(8,128)(2,1)S(1)} %maximum_select_fusion.3), channel_id=1, source_target_pairs={{0,128},{16,144},{32,160},{48,176},{64,192},{80,208},{96,224},{112... | collective-permute-start | bytes 786440 | tf_op jit(solution)/shard_map/ppermute | solution.py:28
  76.0 6.8 %collective-permute-start.13 = (bf16[2,32,8,256]{3,2,1,0:T(8,128)(2,1)S(1)}, bf16[2,32,8,256]{3,2,1,0:T(8,128)(2,1)S(1)}, u32[]{:S(2)}, u32[]{:S(2)}) collective-permute-start(bf16[2,32,8,256]{3,2,1,0:T(8,128)(2,1)S(1)} %maximum_select_fusion.4), channel_id=1, source_target_pairs={{0,128},{16,144},{32,160},{48,176},{64,192},{80,208},{96,224},{112... | collective-permute-start | bytes 786440 | tf_op jit(solution)/shard_map/ppermute | solution.py:28
  83.4 1.0 copy-start
  83.4 1.0 copy-start.2
  83.4 1.0 copy-start.6
  84.4 1.0 copy-start.4
  99.8 1.0 copy-start.8
  101.1 4.2 copy-start.9
  115.6 1.2 copy-start.21
  119.6 1.0 copy-start.5
  120.6 1.0 copy-start.4
  136.1 1.0 copy-start.8
  137.3 4.2 copy-start.9
  151.9 1.2 copy-start.21
  155.9 1.0 copy-start.5
  156.9 0.9 copy-start.1
  156.9 0.9 copy-start.3
  156.9 8.3 %copy-start.10 = (f32[2,32,8,256]{3,2,1,0:T(8,128)S(1)}, f32[2,32,8,256]{3,2,1,0:T(8,128)}, u32[]{:S(2)}) copy-start(f32[2,32,8,256]{3,2,1,0:T(8,128)} %get-tuple-element.133) | copy-start | bytes 1572868
  156.9 8.3 %collective-permute-start.14 = (f32[2,32,8,256]{3,2,1,0:T(8,128)}, f32[2,32,8,256]{3,2,1,0:T(8,128)S(1)}, u32[]{:S(2)}, u32[]{:S(2)}) collective-permute-start(f32[2,32,8,256]{3,2,1,0:T(8,128)} %get-tuple-element.133), channel_id=1, source_target_pairs={{0,128},{16,144},{32,160},{48,176},{64,192},{80,208},{96,224},{112... | collective-permute-start | bytes 1572872 | tf_op jit(solution)/shard_map/ppermute | solution.py:28
  157.8 292.3 %all-reduce.28.cloned.1.call-start = ((), (), s32[]{:S(2)}) async-start(), calls=%async_computation.1 | async-start | bytes 1769472 | tf_op jit(solution)/shard_map/psum | solution.py:227
  165.3 0.8 copy-start.14
  198.6 11.8 %collective-permute-start.15 = (f32[32,4,264]{2,1,0:T(4,128)S(1)}, f32[32,4,264]{2,1,0:T(4,128)S(1)}, u32[]{:S(2)}, u32[]{:S(2)}) collective-permute-start(f32[32,4,264]{2,1,0:T(4,128)S(1)} %get-tuple-element.242), channel_id=1, source_target_pairs={{0,16},{16,32},{32,48},{48,64},{64,80},{80,96},{96,112},{112,128},... | collective-permute-start | bytes 405512 | tf_op jit(solution)/shard_map/ppermute | solution.py:17
  207.8 9.3 %collective-permute-start.16 = (f32[32,4,264]{2,1,0:T(4,128)S(1)}, f32[32,4,264]{2,1,0:T(4,128)S(1)}, u32[]{:S(2)}, u32[]{:S(2)}) collective-permute-start(f32[32,4,264]{2,1,0:T(4,128)S(1)} %get-tuple-element.243), channel_id=1, source_target_pairs={{16,0},{32,16},{48,32},{64,48},{80,64},{96,80},{112,96},{128,112},... | collective-permute-start | bytes 405512 | tf_op jit(solution)/shard_map/ppermute | solution.py:20
  217.3 18.3 %collective-permute-start.17 = (f32[32,24,4]{2,1,0:T(8,128)S(1)}, f32[32,24,4]{2,1,0:T(8,128)S(1)}, u32[]{:S(2)}, u32[]{:S(2)}) collective-permute-start(f32[32,24,4]{2,1,0:T(8,128)S(1)} %get-tuple-element.240), channel_id=1, source_target_pairs={{0,1},{1,2},{2,3},{3,4},{4,5},{5,6},{6,7},{7,8},{8,9},{9,10},{10,1... | collective-permute-start | bytes 36872 | tf_op jit(solution)/shard_map/ppermute | solution.py:17
  217.4 18.2 %collective-permute-start.18 = (f32[32,24,4]{2,1,0:T(8,128)S(1)}, f32[32,24,4]{2,1,0:T(8,128)S(1)}, u32[]{:S(2)}, u32[]{:S(2)}) collective-permute-start(f32[32,24,4]{2,1,0:T(8,128)S(1)} %get-tuple-element.241), channel_id=1, source_target_pairs={{1,0},{2,1},{3,2},{4,3},{5,4},{6,5},{7,6},{8,7},{9,8},{10,9},{11,1... | collective-permute-start | bytes 36872 | tf_op jit(solution)/shard_map/ppermute | solution.py:20
  235.6 0.8 copy-start.11
  235.6 77.9 %copy-start.12 = (f32[32,24,4]{2,1,0:T(8,128)}, f32[32,24,4]{2,1,0:T(8,128)S(1)}, u32[]{:S(2)}) copy-start(f32[32,24,4]{2,1,0:T(8,128)S(1)} %collective-permute-done.18) | copy-start | bytes 36868
  313.7 0.9 slice-start
  313.7 1.0 slice-start.1
  313.7 1.0 copy-start.18
  451.7 2.0 copy-start.15
Sparse Core Ops, SparseCore 0:
  157.9 155.4 all-reduce.25
  316.3 133.8 all-reduce.27
